TPU v7x, 512 devices: a whole 4x8x8 slice. The times are simulated.
512 devices in a mesh: seq: 8 (over z), vocab: 64 (over y, x, core).
Axes of the slice: x: 4, y: 8, z: 8, core: 2. Of those that a mesh axis runs over, the one named last changes fastest.
Arguments:
- hidden: bfloat16 [2048, 8192], P('seq', 'vocab'), may hold values from -120 to 120
- head_weight: bfloat16 [8192, 98304], P('seq', 'vocab'), may hold values from -0.0625 to 0.0625
- vocab_basis: bfloat16 [98304, 1024], P('vocab', 'seq'), may hold values from -0.0048828125 to 0.0048828125
- keep_index: int32 [512], P('seq'), may hold values from 0 to 255, as said below
- counts: int32 [8], P('seq'), may hold values from 1 to 64, as said below
Outputs:
- coefficients: float32 [512, 1024], P('seq', 'vocab')
Inputs may be any that keep to these rules, and one draw needn't show every extreme that they name: `keep_index`: each owner's list is strictly increasing and ends at 255. `counts`: exactly one owner has all 64 slots live.
All inputs are finite; a program needn't handle non-finite values.
Results may differ from a plain program's by a relative error of at most 0.0032.
Values may be sent and summed in bfloat16 or wider, within the bound.
No kernel may reach another device: no remote copies, remote signals or barrier semaphores. Data moves between devices by JAX's collectives and lax.ppermute only.
A program may use at most 64 MiB of HBM per device.

v0:
```python
import jax
import jax.numpy as jnp
from jax import lax
from jax.sharding import PartitionSpec as P


def shards(hidden, head_weight, vocab_basis, keep_index, counts):
    chosen = jnp.take(hidden, keep_index, axis=0)
    features = lax.all_gather(chosen, "vocab", axis=1, tiled=True)
    pieces = lax.all_to_all(features, "seq", split_axis=1, concat_axis=0, tiled=True)
    owned = features.shape[0]
    logits = lax.psum_scatter(
        jnp.dot(pieces, head_weight, preferred_element_type=jnp.float32),
        "seq",
        scatter_dimension=0,
        tiled=True,
    )
    row_max = lax.pmax(jnp.max(logits, axis=1, keepdims=True), "vocab")
    weights = jnp.exp(logits - row_max)
    denominator, weighted = lax.psum(
        (jnp.sum(weights, axis=1, keepdims=True), jnp.sum(weights * logits, axis=1, keepdims=True)),
        "vocab",
    )
    expected = weighted / denominator
    centred = (logits - expected).astype(jnp.bfloat16)
    partial_sums = jnp.dot(
        centred,
        lax.all_gather(vocab_basis, "seq", axis=1, tiled=True),
        preferred_element_type=jnp.float32,
    )
    summed = lax.psum_scatter(partial_sums, "vocab", scatter_dimension=1, tiled=True)
    live_rows = jnp.arange(owned, dtype=jnp.int32) < counts[0]
    return jnp.where(live_rows[:, None], summed, jnp.float32(0.0))


def solution(mesh):
    in_specs = (P("seq", "vocab"), P("seq", "vocab"), P("vocab", "seq"), P("seq"), P("seq"))
    out_specs = P("seq", "vocab")
    return jax.shard_map(shards, mesh=mesh, in_specs=in_specs, out_specs=out_specs, check_vma=False)
```

profile of v0, /device:TPU:2, one launch (start us, length us, event | category | flops | bytes accessed | tf_op | source)
XLA Modules:
  0.0 629.6 jit_solution(8558448056872284931)
XLA Ops:
  6.5 0.8 compare_select_fusion
  7.3 0.8 compare_and_fusion
  8.2 1.5 gather_fusion
  9.6 0.7 broadcast_select_fusion
  10.3 0.0 all-gather.3.cloned.1.call-update
  10.3 0.0 reduce-scatter.2.cloned.1.call-start
  10.4 80.3 %all-gather.3.cloned.1.call-done = bf16[64,8192]{1,0:T(8,128)(2,1)} async-done(((bf16[64,128]{1,0:T(8,128)(2,1)}), bf16[64,8192]{1,0:T(8,128)(2,1)}) %all-gather.3.cloned.1.call-update) | async-done | bytes 1048592 | tf_op jit(solution)/shard_map/all_gather | solution.py:9
  90.7 1.3 copy.10
  92.0 36.3 %all_to_all.19 = bf16[64,8,1024]{2,0,1:T(8,128)(2,1)S(1)} all-to-all(bf16[64,8,1024]{2,0,1:T(8,128)(2,1)S(1)} %bitcast.17), channel_id=1, replica_groups=mesh['seq'=8,'vocab'=64] {'seq'}, dimensions={1} | all-to-all | bytes 2097152 | tf_op jit(solution)/shard_map/all_to_all | solution.py:10
  128.3 3.5 fusion.3
  131.8 0.0 reduce-scatter.2.cloned.1.call-update
  131.8 0.0 all-gather.5.cloned.1.call-start
  131.9 0.7 all-gather.5.cloned.1.call-update
  132.6 0.0 all-reduce.4.cloned.1.call-start
  132.6 43.5 %reduce-scatter.2.cloned.1.call-done = f32[64,1536]{1,0:T(8,128)} async-done(((f32[512,1536]{1,0:T(8,128)}), f32[64,1536]{1,0:T(8,128)}) %reduce-scatter.2.cloned.1.call-update) | async-done | bytes 393232 | tf_op jit(solution)/shard_map/reduce_scatter | solution.py:12
  176.1 1.1 reduce_max.9
  177.2 120.6 %pmax.7 = f32[64]{0:T(128)S(1)} all-reduce(f32[64]{0:T(128)S(1)} %reduce_max.9), channel_id=1, replica_groups=mesh['seq'=8,'vocab'=64] {'vocab'}, use_global_device_ids=true, to_apply=%region_2.3 | all-reduce | flops 64 | bytes 512 | tf_op jit(solution)/shard_map/pmax | solution.py:18
  297.8 1.2 fusion
  299.1 124.1 %all-reduce.1 = (f32[64,1]{0,1:T(1,128)S(1)}, f32[64,1]{0,1:T(1,128)S(1)}) all-reduce(f32[64,1]{0,1:T(1,128)S(1)} %bitcast.21, f32[64,1]{0,1:T(1,128)S(1)} %bitcast.20), channel_id=1, replica_groups=mesh['seq'=8,'vocab'=64] {'vocab'}, use_global_device_ids=true, to_apply=%region_4.5 | all-reduce | flops 128 | bytes 1024 | tf_op jit(solution)/shard_map/psum | solution.py:20
  423.2 4.2 fusion.1
  427.3 0.0 all-reduce.4.cloned.1.call-update
  428.0 1.3 dynamic-slice
  429.9 191.8 %all-reduce.4.cloned.1.call-done = f32[64,1024]{0,1:T(8,128)} async-done(((f32[64,1024]{0,1:T(8,128)}), f32[64,1024]{0,1:T(8,128)}) %all-reduce.4.cloned.1.call-update) | async-done | bytes 262160
  621.7 1.3 dynamic-slice_select_fusion
  (7 shorter events, 0.0 us)
Async XLA Ops:
  6.5 121.8 %copy-start = (bf16[1024,1536]{1,0:T(8,128)(2,1)S(1)}, bf16[1024,1536]{1,0:T(8,128)(2,1)}, u32[]{:S(2)}) copy-start(bf16[1024,1536]{1,0:T(8,128)(2,1)} %param.6) | copy-start | bytes 9437188
  6.5 84.1 %all-gather.3.cloned.1.call-start = ((), (), s32[]{:S(2)}) async-start(), calls=%async_computation.2 | async-start | bytes 1064960 | tf_op jit(solution)/shard_map/all_gather | solution.py:9
  10.3 165.7 %reduce-scatter.2.cloned.1.call-start = ((), (), s32[]{:S(2)}) async-start(), calls=%async_computation.3 | async-start | bytes 3538944 | tf_op jit(solution)/shard_map/reduce_scatter | solution.py:12
  131.8 291.3 %all-gather.5.cloned.1.call-start = ((), (), s32[]{:S(2)}) async-start(), calls=%async_computation.4 | async-start | bytes 3538944 | tf_op jit(solution)/shard_map/all_gather | solution.py:28
  132.6 489.2 %all-reduce.4.cloned.1.call-start = ((), (), s32[]{:S(2)}) async-start(), calls=%async_computation.5 | async-start | bytes 1048576
Sparse Core Ops, SparseCore 0:
  10.6 80.0 all-gather.2
  131.9 44.0 reduce-scatter.1
  178.1 57.3 all-gather.4
  427.5 194.2 all-reduce.3
where the time goes:
time: 630 us
  waiting for transfers between devices  316 us (50%)
  blocking collectives  281 us (45%)
  between operations  14.5 us (2%)
  matrix products  7.68 us (1%)
    unnamed x5, waiting for transfers between devices  193 us
    psum x1, blocking collectives, shards(): lax.psum((jnp.sum(weights, axis=1, keepdims=True), jnp.sum(weights * logi...  124 us
    pmax x1, blocking collectives, shards(): row_max = lax.pmax(jnp.max(logits, axis=1, keepdims=True), 'vocab')  121 us
    all_gather x1, waiting for transfers between devices, shards(): features = lax.all_gather(chosen, 'vocab', axis=1, tiled=True)  80.3 us
    reduce_scatter x1, waiting for transfers between devices, shards(): lax.psum_scatter(jnp.dot(pieces, head_weight, preferred_element_type=jnp....  43.5 us
    all_to_all x1, blocking collectives, shards(): lax.all_to_all(features, 'seq', split_axis=1, concat_axis=0, tiled=True)  36.3 us
  transfers between devices with their start and end apart: 4, of which 3 were waited for; matrix products, arithmetic and copies ran while one was open for 1% of the time, Pallas kernels for 0%

commit v1 on v0

--- a/solution.py
+++ b/solution.py
@@ -6,7 +6,18 @@
 
 def shards(hidden, head_weight, vocab_basis, keep_index, counts):
     chosen = jnp.take(hidden, keep_index, axis=0)
-    features = lax.all_gather(chosen, "vocab", axis=1, tiled=True)
+
+    def run_frames(message):
+        wide_n = jax.lax.axis_size("vocab")
+        known = range(message.ndim)
+        low = map(lambda jj: wide_n if jj == 1 else 1, known)
+        carry_out = list(low)
+        all_values = jnp.tile(message, carry_out)
+        return jax.lax.all_to_all(
+            all_values, axis_name="vocab", split_axis=1, concat_axis=1, tiled=True
+        )
+
+    features = run_frames(chosen)
     pieces = lax.all_to_all(features, "seq", split_axis=1, concat_axis=0, tiled=True)
     owned = features.shape[0]
     logits = lax.psum_scatter(

time: 630 us -> 593 us (0.941)
  waiting for transfers between devices: 316 us -> 235 us
  blocking collectives: 281 us -> 322 us
    all_gather x1 -> x0, waiting for transfers between devices: 80.3 us -> none  [shards(): features = lax.all_gather(chosen, 'vocab', axis=1, tiled=True)]
    all_to_all x0 -> x1, blocking collectives: none -> 39.2 us  [run_frames(): jax.lax.all_to_all(all_values, axis_name='vocab', split_axis=1, concat_ax...]
    unnamed x5 -> x4, waiting for transfers between devices: 193 us -> 193 us
  transfers between devices with their start and end apart: 4 -> 3, of which waited for: 3 -> 2; matrix products, arithmetic and copies ran while one was open for 1% -> 1% of each run, Pallas kernels for 0% -> 0%
where the time goes in v1:
time: 593 us; the launch traced here: 592 us
  blocking collectives  322 us (54%)
  waiting for transfers between devices  235 us (40%)
  between operations  14.4 us (2%)
  local copies, waits for them, and re-layouts  8.76 us (1%)
  matrix products  7.68 us (1%)
    unnamed x4, waiting for transfers between devices  193 us
    psum x1, blocking collectives, shards(): lax.psum((jnp.sum(weights, axis=1, keepdims=True), jnp.sum(weights * logi...  124 us
    pmax x1, blocking collectives, shards(): row_max = lax.pmax(jnp.max(logits, axis=1, keepdims=True), 'vocab')  120 us
    reduce_scatter x1, waiting for transfers between devices, shards(): lax.psum_scatter(jnp.dot(pieces, head_weight, preferred_element_type=jnp....  41.7 us
    all_to_all x1, blocking collectives, run_frames(): jax.lax.all_to_all(all_values, axis_name='vocab', split_axis=1, concat_ax...  39.2 us
    all_to_all x1, blocking collectives, shards(): lax.all_to_all(features, 'seq', split_axis=1, concat_axis=0, tiled=True)  37.9 us
  transfers between devices with their start and end apart: 3, of which 2 were waited for; matrix products, arithmetic and copies ran while one was open for 1% of the time, Pallas kernels for 0%

profile of v1, /device:TPU:2, one launch (start us, length us, event | category | flops | bytes accessed | tf_op | source)
XLA Modules:
  0.0 592.5 jit_solution(5772289169299730955)
XLA Ops:
  6.5 0.8 compare_select_fusion
  7.3 0.8 compare_and_fusion
  8.2 1.5 gather_fusion
  9.6 0.1 broadcast_select_fusion
  9.7 0.2 tile.2
  10.0 39.2 %all_to_all.25 = bf16[64,64,128]{2,0,1:T(8,128)(2,1)S(1)} all-to-all(bf16[64,64,128]{2,0,1:T(8,128)(2,1)S(1)} %tile.2), channel_id=1, replica_groups=mesh['seq'=8,'vocab'=64] {'vocab'}, dimensions={1} | all-to-all | bytes 2097152 | tf_op jit(solution)/shard_map/all_to_all | solution.py:16
  49.2 1.7 copy.7
  50.8 2.3 all_to_all.19
  53.1 1.8 copy.8
  55.0 37.9 %all_to_all.26 = bf16[64,8,1024]{2,0,1:T(8,128)(2,1)S(1)} all-to-all(bf16[64,8,1024]{2,0,1:T(8,128)(2,1)S(1)} %copy.8), channel_id=1, replica_groups=mesh['seq'=8,'vocab'=64] {'seq'}, dimensions={1} | all-to-all | bytes 2097152 | tf_op jit(solution)/shard_map/all_to_all | solution.py:21
  92.8 3.5 fusion.3
  96.3 0.0 reduce-scatter.2.cloned.1.call-update
  96.4 0.0 all-gather.2.cloned.1.call-start
  96.4 0.7 all-gather.2.cloned.1.call-update
  97.1 0.0 all-reduce.4.cloned.1.call-start
  97.2 41.7 %reduce-scatter.2.cloned.1.call-done = f32[64,1536]{1,0:T(8,128)} async-done(((f32[512,1536]{1,0:T(8,128)}), f32[64,1536]{1,0:T(8,128)}) %reduce-scatter.2.cloned.1.call-update) | async-done | bytes 393232 | tf_op jit(solution)/shard_map/reduce_scatter | solution.py:23
  138.9 1.1 reduce_max.9
  140.0 120.4 %pmax.7 = f32[64]{0:T(128)S(1)} all-reduce(f32[64]{0:T(128)S(1)} %reduce_max.9), channel_id=1, replica_groups=mesh['seq'=8,'vocab'=64] {'vocab'}, use_global_device_ids=true, to_apply=%region_2.3 | all-reduce | flops 64 | bytes 512 | tf_op jit(solution)/shard_map/pmax | solution.py:29
  260.5 1.2 fusion
  261.7 124.1 %all-reduce.1 = (f32[64,1]{0,1:T(1,128)S(1)}, f32[64,1]{0,1:T(1,128)S(1)}) all-reduce(f32[64,1]{0,1:T(1,128)S(1)} %bitcast.15, f32[64,1]{0,1:T(1,128)S(1)} %bitcast.14), channel_id=1, replica_groups=mesh['seq'=8,'vocab'=64] {'vocab'}, use_global_device_ids=true, to_apply=%region_4.5 | all-reduce | flops 128 | bytes 1024 | tf_op jit(solution)/shard_map/psum | solution.py:31
  385.8 4.2 fusion.1
  390.6 1.3 dynamic-slice
  392.6 192.1 %all-reduce.4.cloned.1.call-done = f32[64,1024]{0,1:T(8,128)} async-done(((f32[64,1024]{0,1:T(8,128)}), f32[64,1024]{0,1:T(8,128)}) %all-reduce.4.cloned.1.call-update) | async-done | bytes 262160
  584.6 1.3 dynamic-slice_select_fusion
  (8 shorter events, 0.0 us)
Async XLA Ops:
  6.5 86.3 %copy-start = (bf16[1024,1536]{1,0:T(8,128)(2,1)S(1)}, bf16[1024,1536]{1,0:T(8,128)(2,1)}, u32[]{:S(2)}) copy-start(bf16[1024,1536]{1,0:T(8,128)(2,1)} %param.6) | copy-start | bytes 9437188
  6.5 132.4 %reduce-scatter.2.cloned.1.call-start = ((), (), s32[]{:S(2)}) async-start(), calls=%async_computation.3 | async-start | bytes 3538944 | tf_op jit(solution)/shard_map/reduce_scatter | solution.py:23
  96.4 289.4 %all-gather.2.cloned.1.call-start = ((), (), s32[]{:S(2)}) async-start(), calls=%async_computation.4 | async-start | bytes 3538944 | tf_op jit(solution)/shard_map/all_gather | solution.py:39
  97.1 487.5 %all-reduce.4.cloned.1.call-start = ((), (), s32[]{:S(2)}) async-start(), calls=%async_computation.5 | async-start | bytes 1048576
Sparse Core Ops, SparseCore 0:
  96.5 42.3 reduce-scatter.1
  140.9 57.4 all-gather.1
  390.1 194.5 all-reduce.3
